TPU v7x, 256 devices: a whole 4x4x8 slice. The times are simulated.
256 devices in a mesh: feature: 4 (over x), kvhead: 8 (over y, core), seq: 8 (over z).
Axes of the slice: x: 4, y: 4, z: 8, core: 2. Of those that a mesh axis runs over, the one named last changes fastest.
Arguments:
- queries: float32 [2048, 40, 128], P('seq', 'kvhead'), may hold values from -6 to 6
- keys: float32 [2048, 8, 128], P('seq', 'kvhead'), may hold values from -6 to 6
- values: float32 [2048, 8, 128], P('seq', 'kvhead'), may hold values from -6 to 6
- w_out: float32 [5120, 5120], P('kvhead', ('feature', 'seq')), may hold values from -0.078125 to 0.078125
Outputs:
- projected: float32 [2048, 5120], P(('seq', 'feature'), 'kvhead')
All inputs are finite; a program needn't handle non-finite values.
Results may differ from a plain program's by a relative error of at most 0.0003.
Values sent between devices are 32-bit elements; how exact they have to be, the bound alone decides.
A program may use at most 128 MiB of HBM per device.

v0:
```python
import math
import jax
import jax.numpy as jnp
import numpy as np
from jax import lax
from jax.sharding import PartitionSpec as P


def from_everyone(x, axis):
    copies = jnp.broadcast_to(x, (lax.axis_size(axis), *x.shape))
    return lax.all_to_all(copies, axis, split_axis=0, concat_axis=0, tiled=True)


def of_everyone(x, axis):
    everything = from_everyone(x, axis)
    return jnp.sum(everything, axis=0)


def in_blocks(x, dim, count):
    before, after = (x.shape[:dim], x.shape[dim + 1 :])
    return jnp.moveaxis(x.reshape(*before, count, -1, *after), dim, 0)


def summed_on_arrival(x, axis, dim):
    count = lax.axis_size(axis)
    blocks = lax.all_to_all(in_blocks(x, dim, count), axis, 0, 0, tiled=True)
    return jnp.sum(blocks, axis=0)


def expand(vectors, select_first, select_second, factor):
    highest = lax.Precision.HIGHEST
    left = jnp.einsum("...d,df->...f", vectors, select_first, precision=highest)
    right = jnp.einsum("...d,df->...f", vectors, select_second, precision=highest)
    return left * right * factor


def local(queries, keys, values, w_out):
    rows, local_heads, head_size = queries.shape
    kv_local = keys.shape[1]
    group = local_heads // kv_local
    parts = lax.axis_size("feature")
    position = lax.axis_index("feature")
    width = head_size * (head_size + 1) // 2 // parts
    upper_i, upper_j = np.triu_indices(head_size)
    factor_table = np.where(upper_i == upper_j, 1.0, math.sqrt(2.0)).astype(np.float32)
    first = lax.dynamic_slice_in_dim(jnp.asarray(upper_i.astype(np.int32)), position * width, width)
    second = lax.dynamic_slice_in_dim(
        jnp.asarray(upper_j.astype(np.int32)), position * width, width
    )
    factor = lax.dynamic_slice_in_dim(jnp.asarray(factor_table), position * width, width)
    entries = jnp.arange(head_size, dtype=jnp.int32)
    select_first = (entries[:, None] == first[None, :]).astype(jnp.float32)
    select_second = (entries[:, None] == second[None, :]).astype(jnp.float32)
    quarter = rows // parts
    scaled = (queries * head_size ** (-0.5)).reshape(rows, kv_local, group, head_size)
    highest = lax.Precision.HIGHEST
    block_states = []
    block_norms = []
    for block in range(parts):
        key_part = keys[block * quarter : (block + 1) * quarter]
        lifted = expand(key_part, select_first, select_second, factor)
        block_states.append(
            jnp.einsum(
                "tkf,tkd->kfd",
                lifted,
                values[block * quarter : (block + 1) * quarter],
                precision=highest,
            )
        )
        block_norms.append(jnp.sum(lifted, axis=0))
    total_state = sum(block_states)
    total_norm = sum(block_norms)
    own_index = lax.axis_index("seq")
    empty = (jnp.zeros_like(total_state), jnp.zeros_like(total_norm))
    pieces = (
        lax.all_gather(total_state[None], "seq", axis=0, tiled=True),
        lax.all_gather(total_norm[None], "seq", axis=0, tiled=True),
    )
    count = pieces[0].shape[0]
    keep = (jnp.arange(count, dtype=jnp.int32) < own_index).astype(jnp.float32)
    prior_state = empty[0] + jnp.einsum("n,nkfd->kfd", keep, pieces[0], precision=highest)
    prior_norm = empty[1] + jnp.einsum("n,nkf->kf", keep, pieces[1], precision=highest)
    running_state = prior_state
    running_norm = prior_norm
    numerators = []
    denominators = []
    for block in range(parts):
        lifted_query = expand(
            scaled[block * quarter : (block + 1) * quarter], select_first, select_second, factor
        )
        numerators.append(
            jnp.einsum("tkgf,kfd->tkgd", lifted_query, running_state, precision=highest)
        )
        denominators.append(
            jnp.einsum("tkgf,kf->tkg", lifted_query, running_norm, precision=highest)
        )
        running_state = running_state + block_states[block]
        running_norm = running_norm + block_norms[block]
    numerator = jnp.concatenate(numerators, axis=0)
    denominator = jnp.concatenate(denominators, axis=0)
    own_start = position * quarter
    own_query = lax.dynamic_slice_in_dim(scaled, own_start, quarter, 0)
    own_key = lax.dynamic_slice_in_dim(keys, own_start, quarter, 0)
    own_value = lax.dynamic_slice_in_dim(values, own_start, quarter, 0)
    scores = jnp.einsum("tkgd,skd->kgts", own_query, own_key, precision=highest)
    causal = jnp.tril(jnp.ones((quarter, quarter), jnp.bool_))
    squared = jnp.where(causal[None, None], scores * scores, jnp.float32(0.0))
    inner_numerator = jnp.einsum("kgts,skd->tkgd", squared, own_value, precision=highest)
    inner_denominator = jnp.transpose(jnp.sum(squared, axis=-1), (2, 0, 1))
    numerator = lax.dynamic_update_slice_in_dim(
        numerator,
        lax.dynamic_slice_in_dim(numerator, own_start, quarter, 0) + inner_numerator,
        own_start,
        0,
    )
    denominator = lax.dynamic_update_slice_in_dim(
        denominator,
        lax.dynamic_slice_in_dim(denominator, own_start, quarter, 0) + inner_denominator,
        own_start,
        0,
    )
    whole_numerator, whole_denominator = (
        of_everyone(numerator, "feature"),
        of_everyone(denominator, "feature"),
    )
    share_numerator = lax.dynamic_slice_in_dim(whole_numerator, own_start, quarter, 0)
    share_denominator = lax.dynamic_slice_in_dim(whole_denominator, own_start, quarter, 0)
    attended = (share_numerator / (share_denominator[..., None] + 1.0)).reshape(
        quarter, local_heads * head_size
    )
    partial_out = jnp.dot(
        attended,
        lax.all_gather(w_out, ("feature", "seq"), axis=1, tiled=True),
        precision=highest,
        preferred_element_type=jnp.float32,
    )
    return summed_on_arrival(partial_out, "kvhead", 1)


def solution(mesh):
    in_specs = (
        P("seq", "kvhead", None),
        P("seq", "kvhead", None),
        P("seq", "kvhead", None),
        P("kvhead", ("feature", "seq")),
    )
    out_specs = P(("seq", "feature"), "kvhead")
    return jax.shard_map(local, mesh=mesh, in_specs=in_specs, out_specs=out_specs, check_vma=False)
```

profile of v0, /device:TPU:1, one launch (start us, length us, event | category | flops | bytes accessed | tf_op | source)
XLA Modules:
  0.0 359.7 jit_solution(14535412155245520975)
XLA Ops:
  20.6 1.9 fusion.90
  22.4 1.9 fusion.89
  26.2 2.9 convolution_add_fusion
  37.1 3.1 fusion.2
  40.2 3.1 fusion.3
  43.4 3.1 fusion.4
  46.5 3.0 fusion.5
  49.5 40.5 %all-reduce.3.cloned.1.call-done = f32[16512]{0:T(1024)} async-done(((f32[16512]{0:T(1024)}), f32[16512]{0:T(1024)}) %all-reduce.3.cloned.1.call-update) | async-done | bytes 66064
  91.3 5.7 %convolution_bitcast_fusion.6 = f32[64,1,5]{0,1,2:T(1,128)S(1)} fusion(f32[2064,1,1]{0,1,2:T(1,128)S(1)} %reshape.303, f32[64,5,2064]{2,0,1:T(8,128)} %fusion.2), kind=kOutput, calls=%fused_computation.31 | convolution fusion | flops 7925760 | bytes 2651456 | tf_op jit(solution)/shard_map/tkgf,kf->tkg/dot_general | solution.py:95
  97.0 3.3 convolution_bitcast_fusion.7
  100.3 3.3 convolution_bitcast_fusion.8
  103.6 3.3 convolution_bitcast_fusion.9
  108.0 4.1 %all-to-all-start.1 = ((f32[4,256,1,5]{1,2,3,0:T(1,128)}), f32[4,256,1,5]{1,2,3,0:T(1,128)S(1)}, u32[]{:S(2)}, u32[]{:S(2)}) async-start(f32[4,256,1,5]{1,2,3,0:T(1,128)} %broadcast_in_dim.20), calls=%async_computation.1 | async-start | bytes 40960 | tf_op jit(solution)/shard_map/all_to_all | solution.py:11
  112.1 77.6 %all-gather.7.cloned.1.call-done = f32[16512,128]{1,0:T(8,128)} async-done(((f32[2064,128]{1,0:T(8,128)}), f32[16512,128]{1,0:T(8,128)}) %all-gather.7.cloned.1.call-update) | async-done | bytes 8454160 | tf_op jit(solution)/shard_map/all_gather | solution.py:76
  189.7 9.6 %fusion = f32[1,2064,128]{2,0,1:T(1,128)S(1)} fusion(f32[8,2064,128]{2,1,0:T(8,128)} %bitcast.154, s32[]{:T(128)S(6)} %axis_index.22), kind=kOutput, calls=%fused_computation | convolution fusion | flops 25362440 | bytes 9510916 | tf_op jit(solution)/shard_map/n,nkfd->kfd/dot_general | solution.py:81
  199.3 2.4 convolution_bitcast_fusion.5
  201.8 2.4 convolution_bitcast_fusion.4
  204.2 2.7 convolution_bitcast_fusion.3
  206.9 2.5 convolution_bitcast_fusion.2
  211.8 4.0 %all-to-all-start = ((f32[4,256,1,5,128]{4,1,3,2,0:T(8,128)}), f32[4,256,1,5,128]{4,1,3,2,0:T(8,128)S(1)}, u32[]{:S(2)}, u32[]{:S(2)}) async-start(f32[4,256,1,5,128]{4,1,3,2,0:T(8,128)} %broadcast_in_dim.19), calls=%async_computation | async-start | bytes 5242880 | tf_op jit(solution)/shard_map/all_to_all | solution.py:11
  215.8 32.7 %all-to-all-done = f32[4,256,1,5,128]{4,1,3,2,0:T(8,128)S(1)} async-done(((f32[4,256,1,5,128]{4,1,3,2,0:T(8,128)}), f32[4,256,1,5,128]{4,1,3,2,0:T(8,128)S(1)}, u32[]{:S(2)}, u32[]{:S(2)}) %all-to-all-start) | async-done | bytes 2621472 | tf_op jit(solution)/shard_map/all_to_all | solution.py:11
  249.1 64.6 %all-gather.5.cloned.1.call-done = f32[640,5120]{0,1:T(8,128)} async-done(((f32[640,160]{0,1:T(8,128)}), f32[640,5120]{0,1:T(8,128)}) %all-gather.5.cloned.1.call-update) | async-done | bytes 13107216 | tf_op jit(solution)/shard_map/all_gather | solution.py:133
  313.6 15.7 %convolution_bitcast_fusion = f32[8,64,640]{2,1,0:T(8,128)S(1)} fusion(f32[64,640,1]{1,0,2:T(8,128)S(1)} %reshape.305, f32[8,640,640]{2,1,0:T(8,128)} %bitcast.153), kind=kOutput, calls=%fused_computation.19 | convolution fusion | flops 2516582400 | bytes 14581760 | tf_op jit(solution)/shard_map/dot_general | solution.py:131
  329.4 22.8 %all_to_all.15 = f32[8,64,640]{2,1,0:T(8,128)S(1)} all-to-all(f32[8,64,640]{2,1,0:T(8,128)S(1)} %convolution_bitcast_fusion), channel_id=1, replica_groups=mesh['feature'=4,'kvhead'=8,'seq'=8] {'kvhead'}, dimensions={0} | all-to-all | bytes 2621440 | tf_op jit(solution)/shard_map/all_to_all | solution.py:26
  (77 shorter events, 28.9 us)
Async XLA Ops:
  6.5 83.5 %all-reduce.3.cloned.1.call-start = ((), (), s32[]{:S(2)}) async-start(), calls=%async_computation.5 | async-start | bytes 139264
  15.7 2.5 copy-start.11
  15.7 4.8 %copy-start.10 = (f32[256,1,128]{2,1,0:T(1,128)S(1)}, f32[256,1,128]{2,1,0:T(1,128)}, u32[]{:S(2)}) copy-start(f32[256,1,128]{2,1,0:T(1,128)} %param.9) | copy-start | bytes 393220
  19.6 0.6 copy-start.9
  20.3 169.4 %all-gather.7.cloned.1.call-start = ((), (), s32[]{:S(2)}) async-start(), calls=%async_computation.4 | async-start | bytes 9510912 | tf_op jit(solution)/shard_map/all_gather | solution.py:76
  22.4 1.9 copy-start.8
  24.3 1.9 copy-start.7
  29.2 284.5 %all-gather.5.cloned.1.call-start = ((), (), s32[]{:S(2)}) async-start(), calls=%async_computation.3 | async-start | bytes 13516800 | tf_op jit(solution)/shard_map/all_gather | solution.py:133
  91.3 5.7 %copy-start.1 = (f32[64,5,2064]{2,0,1:T(8,128)S(1)}, f32[64,5,2064]{2,0,1:T(8,128)}, u32[]{:S(2)}) copy-start(f32[64,5,2064]{2,0,1:T(8,128)} %fusion.3) | copy-start | bytes 7925764
  96.9 3.3 copy-start.3
  100.3 3.3 copy-start.5
  108.0 102.0 %all-to-all-start.1 = ((f32[4,256,1,5]{1,2,3,0:T(1,128)}), f32[4,256,1,5]{1,2,3,0:T(1,128)S(1)}, u32[]{:S(2)}, u32[]{:S(2)}) async-start(f32[4,256,1,5]{1,2,3,0:T(1,128)} %broadcast_in_dim.20), calls=%async_computation.1 | async-start | bytes 40960 | tf_op jit(solution)/shard_map/all_to_all | solution.py:11
  189.7 9.6 %copy-start.6 = (f32[64,5,2064]{2,0,1:T(8,128)S(1)}, f32[64,5,2064]{2,0,1:T(8,128)}, u32[]{:S(2)}) copy-start(f32[64,5,2064]{2,0,1:T(8,128)} %fusion.5) | copy-start | bytes 7925764
  199.3 2.4 copy-start.4
  201.7 2.4 copy-start.2
  204.2 2.7 copy-start
  211.8 36.8 %all-to-all-start = ((f32[4,256,1,5,128]{4,1,3,2,0:T(8,128)}), f32[4,256,1,5,128]{4,1,3,2,0:T(8,128)S(1)}, u32[]{:S(2)}, u32[]{:S(2)}) async-start(f32[4,256,1,5,128]{4,1,3,2,0:T(8,128)} %broadcast_in_dim.19), calls=%async_computation | async-start | bytes 5242880 | tf_op jit(solution)/shard_map/all_to_all | solution.py:11
Sparse Core Ops, SparseCore 0:
  20.4 69.5 all-reduce.2
  91.8 97.8 all-gather.6
  192.3 121.2 all-gather.4
where the time goes:
time: 365 us; the launch traced here: 360 us
  waiting for transfers between devices  216 us (59%)
  matrix products  87.1 us (24%)
  blocking collectives  22.8 us (6%)
  between operations  14.4 us (4%)
  starting transfers between devices  8.51 us (2%)
  local copies, waits for them, and re-layouts  8.29 us (2%)
    all_gather x1, waiting for transfers between devices, local(): lax.all_gather(total_state[None], 'seq', axis=0, tiled=True)  77.6 us
    all_gather x1, waiting for transfers between devices, local(): lax.all_gather(w_out, ('feature', 'seq'), axis=1, tiled=True)  64.6 us
    unnamed x4, waiting for transfers between devices  41 us
    all_to_all x2, waiting for transfers between devices, from_everyone(): return lax.all_to_all(copies, axis, split_axis=0, concat_axis=0, tiled=True)  32.7 us
    all_to_all x1, blocking collectives, summed_on_arrival(): blocks = lax.all_to_all(in_blocks(x, dim, count), axis, 0, 0, tiled=True)  22.8 us
    dot_general x8, matrix products, expand(): jnp.einsum('...d,df->...f', vectors, select_second, precision=highest)  17.4 us
    dot_general x1, matrix products, local(): jnp.dot(attended, lax.all_gather(w_out, ('feature', 'seq'), axis=1, tiled...  15.7 us
    dot_general x4, matrix products, local(): jnp.einsum('tkgf,kf->tkg', lifted_query, running_norm, precision=highest)  15.7 us
  transfers between devices with their start and end apart: 5, of which 4 were waited for; matrix products, arithmetic and copies ran while one was open for 19% of the time, Pallas kernels for 0%

commit v1 on v0

--- a/solution.py
+++ b/solution.py
@@ -4,6 +4,16 @@
 import numpy as np
 from jax import lax
 from jax.sharding import PartitionSpec as P
+
+
+def try_all_the_samples_all(d0, inp):
+    current_value = jnp.concatenate(
+        lax.all_to_all(
+            jnp.stack([inp] * lax.axis_size(("feature", "seq")), axis=0), ("feature", "seq"), 0, 0
+        ),
+        axis=d0,
+    )
+    return current_value
 
 
 def from_everyone(x, axis):
@@ -130,7 +140,7 @@
     )
     partial_out = jnp.dot(
         attended,
-        lax.all_gather(w_out, ("feature", "seq"), axis=1, tiled=True),
+        try_all_the_samples_all(1, w_out),
         precision=highest,
         preferred_element_type=jnp.float32,
     )

time: 365 us -> 617 us (1.69)
  the two profiles are of different devices: /device:TPU:1 before, /device:TPU:166 now
where the time goes in v1:
time: 617 us; the launch traced here: 612 us
  waiting for transfers between devices  423 us (69%)
  matrix products  87.3 us (14%)
  blocking collectives  57.3 us (9%)
  between operations  14.7 us (2%)
  starting transfers between devices  13.7 us (2%)
  local copies, waits for them, and re-layouts  13 us (2%)
    all_to_all x1, waiting for transfers between devices, try_all_the_samples_all(): lax.all_to_all(jnp.stack([inp] * lax.axis_size(('feature', 'seq')), axis=...  310 us
    all_gather x1, waiting for transfers between devices, local(): lax.all_gather(total_state[None], 'seq', axis=0, tiled=True)  73.3 us
    unnamed x3, waiting for transfers between devices  40.1 us
    all_to_all x1, blocking collectives, from_everyone(): return lax.all_to_all(copies, axis, split_axis=0, concat_axis=0, tiled=True)  34.4 us
    all_to_all x1, blocking collectives, summed_on_arrival(): blocks = lax.all_to_all(in_blocks(x, dim, count), axis, 0, 0, tiled=True)  22.9 us
    dot_general x8, matrix products, expand(): jnp.einsum('...d,df->...f', vectors, select_second, precision=highest)  17.5 us
    dot_general x1, matrix products, local(): jnp.dot(attended, try_all_the_samples_all(1, w_out), precision=highest, p...  15.7 us
    dot_general x4, matrix products, local(): jnp.einsum('tkgf,kf->tkg', lifted_query, running_norm, precision=highest)  15.5 us
  transfers between devices with their start and end apart: 4, of which 3 were waited for; matrix products, arithmetic and copies ran while one was open for 11% of the time, Pallas kernels for 0%

profile of v1, /device:TPU:166, one launch (start us, length us, event | category | flops | bytes accessed | tf_op | source)
XLA Modules:
  0.0 611.8 jit_solution(4481353330775592442)
XLA Ops:
  22.4 1.9 fusion.89
  26.2 2.9 convolution_add_fusion
  36.8 3.1 fusion.2
  39.9 3.2 fusion.3
  43.1 3.1 fusion.4
  46.2 3.1 fusion.5
  49.2 40.1 %all-reduce.3.cloned.1.call-done = f32[16512]{0:T(1024)} async-done(((f32[16512]{0:T(1024)}), f32[16512]{0:T(1024)}) %all-reduce.3.cloned.1.call-update) | async-done | bytes 66064
  90.6 5.3 convolution_bitcast_fusion.6
  95.9 3.3 convolution_bitcast_fusion.7
  99.2 3.5 convolution_bitcast_fusion.8
  102.7 3.3 convolution_bitcast_fusion.9
  107.1 4.7 all-to-all-start.1
  111.8 73.3 %all-gather.4.cloned.1.call-done = f32[16512,128]{1,0:T(8,128)} async-done(((f32[2064,128]{1,0:T(8,128)}), f32[16512,128]{1,0:T(8,128)}) %all-gather.4.cloned.1.call-update) | async-done | bytes 8454160 | tf_op jit(solution)/shard_map/all_gather | solution.py:86
  185.1 9.6 %fusion = f32[1,2064,128]{2,0,1:T(1,128)S(1)} fusion(f32[8,2064,128]{2,1,0:T(8,128)} %bitcast.157, s32[]{:T(128)S(6)} %axis_index.22), kind=kOutput, calls=%fused_computation | convolution fusion | flops 25362440 | bytes 9510916 | tf_op jit(solution)/shard_map/n,nkfd->kfd/dot_general | solution.py:91
  194.7 2.5 convolution_bitcast_fusion.2
  197.3 2.5 convolution_bitcast_fusion.3
  199.8 2.6 convolution_bitcast_fusion.4
  202.4 2.4 convolution_bitcast_fusion.5
  205.7 34.4 %all_to_all.20 = f32[4,256,1,5,128]{4,1,3,2,0:T(8,128)S(1)} all-to-all(f32[4,256,1,5,128]{4,1,3,2,0:T(8,128)S(1)} %broadcast_in_dim.19), channel_id=1, replica_groups=mesh['feature'=4,'kvhead'=8,'seq'=8] {'feature'}, dimensions={0} | all-to-all | bytes 5242880 | tf_op jit(solution)/shard_map/all_to_all | solution.py:21
  240.1 6.2 %stack.2 = f32[32,640,160]{1,2,0:T(8,128)} broadcast(f32[640,160]{0,1:T(8,128)S(1)} %copy-done.9), dimensions={1,2} | broadcast | bytes 13516800 | tf_op jit(solution)/shard_map/stack | solution.py:12
  246.3 8.8 %all-to-all-start.2 = ((f32[32,640,160]{1,2,0:T(8,128)}), f32[32,640,160]{1,2,0:T(8,128)}, u32[]{:S(2)}, u32[]{:S(2)}) async-start(f32[32,640,160]{1,2,0:T(8,128)} %stack.2), calls=%async_computation.2 | async-start | bytes 26214400 | tf_op jit(solution)/shard_map/all_to_all | solution.py:11
  255.7 309.7 %all-to-all-done.2 = f32[32,640,160]{1,2,0:T(8,128)} async-done(((f32[32,640,160]{1,2,0:T(8,128)}), f32[32,640,160]{1,2,0:T(8,128)}, u32[]{:S(2)}, u32[]{:S(2)}) %all-to-all-start.2) | async-done | bytes 13107232 | tf_op jit(solution)/shard_map/all_to_all | solution.py:11
  565.4 15.7 %convolution_bitcast_fusion = f32[8,64,640]{2,1,0:T(8,128)S(1)} fusion(f32[64,640,1]{1,0,2:T(8,128)S(1)} %reshape.315, f32[8,640,640]{2,1,0:T(8,128)} %bitcast.49), kind=kOutput, calls=%fused_computation.19 | convolution fusion | flops 2516582400 | bytes 14581760 | tf_op jit(solution)/shard_map/dot_general | solution.py:141
  581.2 22.9 %all_to_all.21 = f32[8,64,640]{2,1,0:T(8,128)S(1)} all-to-all(f32[8,64,640]{2,1,0:T(8,128)S(1)} %convolution_bitcast_fusion), channel_id=1, replica_groups=mesh['feature'=4,'kvhead'=8,'seq'=8] {'kvhead'}, dimensions={0} | all-to-all | bytes 2621440 | tf_op jit(solution)/shard_map/all_to_all | solution.py:36
  (78 shorter events, 29.0 us)
Async XLA Ops:
  6.5 82.8 %all-reduce.3.cloned.1.call-start = ((), (), s32[]{:S(2)}) async-start(), calls=%async_computation.5 | async-start | bytes 139264
  15.7 2.5 copy-start.12
  15.7 4.8 copy-start.11
  19.6 0.6 copy-start.10
  20.3 164.8 %all-gather.4.cloned.1.call-start = ((), (), s32[]{:S(2)}) async-start(), calls=%async_computation.4 | async-start | bytes 9510912 | tf_op jit(solution)/shard_map/all_gather | solution.py:86
  22.4 1.9 copy-start.8
  24.3 1.9 copy-start.7
  90.6 5.3 copy-start.4
  95.9 3.3 copy-start
  99.2 3.5 copy-start.2
  107.1 98.3 %all-to-all-start.1 = ((f32[4,256,1,5]{1,2,3,0:T(1,128)}), f32[4,256,1,5]{1,2,3,0:T(1,128)S(1)}, u32[]{:S(2)}, u32[]{:S(2)}) async-start(f32[4,256,1,5]{1,2,3,0:T(1,128)} %broadcast_in_dim.20), calls=%async_computation.1 | async-start | bytes 40960 | tf_op jit(solution)/shard_map/all_to_all | solution.py:21
  185.1 9.6 %copy-start.6 = (f32[64,5,2064]{2,0,1:T(8,128)S(1)}, f32[64,5,2064]{2,0,1:T(8,128)}, u32[]{:S(2)}) copy-start(f32[64,5,2064]{2,0,1:T(8,128)} %fusion.2) | copy-start | bytes 7925764
  194.7 2.5 copy-start.5
  197.3 2.5 copy-start.1
  199.8 2.7 copy-start.3
  205.7 34.4 %copy-start.9 = (f32[640,160]{0,1:T(8,128)S(1)}, f32[640,160]{0,1:T(8,128)}, u32[]{:S(2)}) copy-start(f32[640,160]{0,1:T(8,128)} %param.10) | copy-start | bytes 1228804
  246.3 319.1 %all-to-all-start.2 = ((f32[32,640,160]{1,2,0:T(8,128)}), f32[32,640,160]{1,2,0:T(8,128)}, u32[]{:S(2)}, u32[]{:S(2)}) async-start(f32[32,640,160]{1,2,0:T(8,128)} %stack.2), calls=%async_computation.2 | async-start | bytes 26214400 | tf_op jit(solution)/shard_map/all_to_all | solution.py:11
Sparse Core Ops, SparseCore 0:
  20.4 68.9 all-reduce.2
  91.1 93.9 all-gather.3
